TPU v7x, 32 devices: a whole 2x2x4 slice. The times are simulated.
32 devices in a mesh: pole: 2 (over x), row: 8 (over z, y), col: 2 (over core).
Axes of the slice: x: 2, y: 2, z: 4, core: 2. Of those that a mesh axis runs over, the one named last changes fastest.
Arguments:
- ancestor_inverse: float32 [2, 24576, 12288], P(None, ('pole', 'row'), 'col'), parts along dimension 1, may hold values from -6 to 6
- factor_panels: float32 [4, 2, 24576, 128], P(None, None, ('pole', 'col', 'row')), parts along dimension 2, may hold values from -0.0546875 to 0.0546875
- diag_inverse: float32 [8, 2, 128, 128], P('pole'), parts along dimension 0, may hold values from -6 to 6
- coupling: float32 [4, 2, 128, 128], P('pole'), parts along dimension 0, may hold values from -0.5 to 0.5
- block_pattern: int32 [4, 96], replicated, may hold values from 0 to 1, as said below
- tree_order: int32 [4], replicated, may hold values from 0 to 3, each once
Outputs:
- inverse_panels: float32 [4, 2, 24576, 128], P(None, None, ('pole', 'row')), parts along dimension 2
- inverse_diagonal: float32 [8, 2, 128, 128], P('pole'), parts along dimension 0
- inverse_coupling: float32 [4, 2, 128, 128], P('pole'), parts along dimension 0
There are 2 independent parts, one for each index of `pole`. A program takes and returns all parts, laid end to end along the dimension named above; an argument that names none is the same for every part. Nothing has to cross between parts.
Inputs may be any that keep to these rules, and one draw needn't show every extreme that they name: `tree_order`: each supernode number appears once. `block_pattern`: blocks 0 and 48 lie in every supernode's structure.
All inputs are finite; a program needn't handle non-finite values.
Results may differ from a plain program's by a relative error of at most 0.0001.
Values sent between devices are 32-bit elements; how exact they have to be, the bound alone decides.
A program may use at most 192 MiB of HBM per device.

v0:
```python
import jax
import jax.numpy as jnp
from jax import lax
from jax.sharding import PartitionSpec as P


def swapped(block, axis, bit):
    count = lax.axis_size(axis)
    route = []
    for low in range(count):
        high = low | 1 << bit
        if high != low and high < count:
            route += [(low, high), (high, low)]
    return lax.ppermute(block, axis, route)


def matmul(left_side, right_side):
    return jnp.dot(
        left_side, right_side, preferred_element_type=jnp.float32, precision=lax.Precision.HIGHEST
    )


def multiply(left_side, right_side):
    real_part = matmul(left_side[0], right_side[0]) - matmul(left_side[1], right_side[1])
    imag_part = matmul(left_side[0], right_side[1]) + matmul(left_side[1], right_side[0])
    return jnp.stack([real_part, imag_part])


def flipped(matrix):
    return jnp.swapaxes(matrix, 1, 2)


def row_masks(pattern_eff, first_row, row_count, block_rows):
    row_index = first_row + jnp.arange(row_count, dtype=jnp.int32)
    blocks = row_index // block_rows
    onehot = (blocks[:, None] == jnp.arange(pattern_eff.shape[1], dtype=jnp.int32)[None, :]).astype(
        jnp.float32
    )
    return matmul(pattern_eff, onehot.T)


def per_device(ancestor_inverse, factor_panels, diag_inverse, coupling, block_pattern, tree_order):
    grid_row = lax.axis_index("row")
    grid_col = lax.axis_index("col")
    tile_rows = ancestor_inverse.shape[1]
    half_rows = ancestor_inverse.shape[2]
    piece_rows = factor_panels.shape[2]
    block_rows = factor_panels.shape[3]
    super_count = factor_panels.shape[0]
    share_rows = tile_rows // 2
    sorted_pattern = jnp.take(block_pattern, tree_order, axis=0).astype(jnp.float32)
    pattern_eff = jnp.concatenate(
        [sorted_pattern[:2], sorted_pattern[2:] * sorted_pattern[:2]], axis=0
    )
    source_mask = row_masks(
        pattern_eff, grid_col * half_rows + grid_row * piece_rows, piece_rows, block_rows
    )
    target_mask = row_masks(pattern_eff, grid_row * tile_rows, tile_rows, block_rows)
    panels = jnp.take(factor_panels, tree_order, axis=0) * source_mask[:, None, :, None]
    diag_blocks = jnp.take(diag_inverse, tree_order, axis=0)
    columns = []
    products = []
    for tree_slot in range(super_count):
        gathered = lax.all_gather(panels[tree_slot], "row", axis=1, tiled=True)
        columns.append(gathered)
        products.append(lax.psum(multiply(ancestor_inverse, gathered), "col"))
    own_flag = (grid_row * tile_rows // half_rows == grid_col).astype(jnp.float32)
    offset = jnp.clip(grid_row * tile_rows - grid_col * half_rows, 0, half_rows - tile_rows)
    own_windows = jnp.stack(
        [
            lax.dynamic_slice_in_dim(column_set, offset, tile_rows, 1) * own_flag
            for column_set in columns
        ]
    )
    partner_windows = swapped(own_windows, "col", 0)
    tile_windows = own_windows + partner_windows

    def share(matrix):
        return lax.dynamic_slice_in_dim(matrix, grid_col * share_rows, share_rows, 1)

    windows = [share(tile_windows[tree_slot]) for tree_slot in range(super_count)]
    parent_cols = [
        -target_mask[tree_slot][None, :, None] * products[tree_slot] for tree_slot in range(2)
    ]
    child_cols = [
        -target_mask[tree_slot + 2][None, :, None]
        * (products[tree_slot + 2] + multiply(parent_cols[tree_slot], coupling[tree_slot]))
        for tree_slot in range(2)
    ]
    parent_local = [
        multiply(flipped(windows[tree_slot]), share(parent_cols[tree_slot]))
        for tree_slot in range(2)
    ]
    cross_local = [
        multiply(flipped(share(parent_cols[tree_slot])), windows[tree_slot + 2])
        for tree_slot in range(2)
    ]
    child_local = [
        multiply(flipped(windows[tree_slot + 2]), share(child_cols[tree_slot]))
        for tree_slot in range(2)
    ]
    parent_sums = lax.psum(jnp.stack(parent_local), ("row", "col"))
    parent_diag = [diag_blocks[tree_slot] - parent_sums[tree_slot] for tree_slot in range(2)]
    child_totals = lax.psum(jnp.stack(cross_local + child_local), ("row", "col"))
    crosses = [
        -(child_totals[tree_slot] + multiply(parent_diag[tree_slot], coupling[tree_slot]))
        for tree_slot in range(2)
    ]
    child_sums = [child_totals[2 + tree_slot] for tree_slot in range(2)]
    child_diag = [
        diag_blocks[tree_slot + 2]
        - child_sums[tree_slot]
        - multiply(flipped(coupling[tree_slot]), crosses[tree_slot])
        for tree_slot in range(2)
    ]
    all_cols = jnp.stack(parent_cols + child_cols)
    all_diag = jnp.stack(parent_diag + child_diag)
    inverse_panels = jnp.zeros_like(all_cols).at[tree_order].set(all_cols)
    inverse_diagonal = jnp.zeros_like(all_diag).at[tree_order].set(all_diag)
    return (inverse_panels, inverse_diagonal, jnp.stack(crosses))


def solution(mesh):
    return jax.shard_map(
        per_device,
        mesh=mesh,
        in_specs=(
            P(None, ("pole", "row"), "col"),
            P(None, None, ("pole", "col", "row"), None),
            P("pole", None, None, None),
            P("pole", None, None, None),
            P(),
            P(),
        ),
        out_specs=(
            P(None, None, ("pole", "row"), None),
            P("pole", None, None, None),
            P("pole", None, None, None),
        ),
        check_vma=False,
    )
```

profile of v0, /device:TPU:0, one launch (start us, length us, event | category | flops | bytes accessed | tf_op | source)
XLA Modules:
  0.0 873.5 jit_solution(7536772676169645142)
XLA Ops:
  9.3 1.2 gather_fusion
  10.7 2.4 gather_fusion.1
  13.5 2.4 select_multiply_fusion
  15.8 1.7 fusion.222
  19.7 99.5 %all-gather.11.cloned.1.call-done = f32[1,2,6144,128]{3,2,1,0:T(8,128)} async-done(((f32[1,2,768,128]{3,2,1,0:T(8,128)}), f32[1,2,6144,128]{3,2,1,0:T(8,128)}) %all-gather.11.cloned.1.call-update) | async-done | bytes 6291472 | tf_op jit(solution)/shard_map/all_gather | solution.py:64
  119.2 36.1 %fusion.8 = f32[128,1536]{1,0:T(8,128)S(1)} fusion(f32[2,1536,6144]{2,1,0:T(8,128)} %param.6, f32[1,2,6144,128]{3,2,1,0:T(8,128)} %all-gather.11.cloned.1.call-done), kind=kOutput, calls=%fused_computation.13 | convolution fusion | flops 14495514624 | bytes 41680896 | tf_op jit(solution)/shard_map/dot_general | solution.py:18
  155.3 35.0 %fusion.10 = f32[128,1536]{1,0:T(8,128)S(1)} fusion(f32[2,1536,6144]{2,1,0:T(8,128)} %param.6, f32[1,2,6144,128]{3,2,1,0:T(8,128)S(1)} %copy-done.2), kind=kOutput, calls=%fused_computation.15 | convolution fusion | flops 14495514624 | bytes 41680896 | tf_op jit(solution)/shard_map/dot_general | solution.py:18
  190.3 35.3 %fusion.73 = f32[1,1536,128]{1,2,0:T(8,128)S(1)} fusion(f32[128,1536]{1,0:T(8,128)S(1)} %fusion.8, f32[2,1536,6144]{2,1,0:T(8,128)} %param.6, f32[1,2,6144,128]{3,2,1,0:T(8,128)S(1)} %copy-done.2), kind=kOutput, calls=%fused_computation.79 | convolution fusion | flops 14495711232 | bytes 42467328 | tf_op jit(solution)/shard_map/dot_general | solution.py:18
  225.6 35.6 %fusion.67 = f32[1,1536,128]{1,2,0:T(8,128)S(1)} fusion(f32[128,1536]{1,0:T(8,128)S(1)} %fusion.10, f32[2,1536,6144]{2,1,0:T(8,128)} %param.6, f32[1,2,6144,128]{3,2,1,0:T(8,128)S(1)} %copy-done.2), kind=kOutput, calls=%fused_computation.77 | convolution fusion | flops 14495711232 | bytes 42467328 | tf_op jit(solution)/shard_map/dot_general | solution.py:18
  261.3 36.6 %fusion.4 = f32[128,1536]{1,0:T(8,128)S(1)} fusion(f32[2,1536,6144]{2,1,0:T(8,128)} %param.6, f32[1,2,6144,128]{3,2,1,0:T(8,128)} %all-gather.13.cloned.1.call-done), kind=kOutput, calls=%fused_computation.9 | convolution fusion | flops 14495514624 | bytes 41680896 | tf_op jit(solution)/shard_map/dot_general | solution.py:18
  297.9 35.2 %fusion.6 = f32[128,1536]{1,0:T(8,128)S(1)} fusion(f32[2,1536,6144]{2,1,0:T(8,128)} %param.6, f32[1,2,6144,128]{3,2,1,0:T(8,128)S(1)} %copy-done.3), kind=kOutput, calls=%fused_computation.11 | convolution fusion | flops 14495514624 | bytes 41680896 | tf_op jit(solution)/shard_map/dot_general | solution.py:18
  333.0 1.3 pad_maximum_fusion.3
  334.4 35.2 %fusion.85 = f32[1,1536,128]{1,2,0:T(8,128)S(1)} fusion(f32[128,1536]{1,0:T(8,128)S(1)} %fusion.4, f32[2,1536,6144]{2,1,0:T(8,128)} %param.6, f32[1,2,6144,128]{3,2,1,0:T(8,128)S(1)} %copy-done.3), kind=kOutput, calls=%fused_computation.83 | convolution fusion | flops 14495711232 | bytes 42467328 | tf_op jit(solution)/shard_map/dot_general | solution.py:18
  369.6 35.0 %fusion.79 = f32[1,1536,128]{1,2,0:T(8,128)S(1)} fusion(f32[128,1536]{1,0:T(8,128)S(1)} %fusion.6, f32[2,1536,6144]{2,1,0:T(8,128)} %param.6, f32[1,2,6144,128]{3,2,1,0:T(8,128)S(1)} %copy-done.3), kind=kOutput, calls=%fused_computation.81 | convolution fusion | flops 14495711232 | bytes 42467328 | tf_op jit(solution)/shard_map/dot_general | solution.py:18
  404.7 1.3 pad_maximum_fusion.4
  405.9 36.3 %fusion = f32[128,1536]{1,0:T(8,128)S(1)} fusion(f32[2,1536,6144]{2,1,0:T(8,128)} %param.6, f32[1,2,6144,128]{3,2,1,0:T(8,128)} %all-gather.15.cloned.1.call-done), kind=kOutput, calls=%fused_computation.5 | convolution fusion | flops 14495514624 | bytes 41680896 | tf_op jit(solution)/shard_map/dot_general | solution.py:18
  442.3 35.0 %fusion.2 = f32[128,1536]{1,0:T(8,128)S(1)} fusion(f32[2,1536,6144]{2,1,0:T(8,128)} %param.6, f32[1,2,6144,128]{3,2,1,0:T(8,128)S(1)} %copy-done.4), kind=kOutput, calls=%fused_computation.7 | convolution fusion | flops 14495514624 | bytes 41680896 | tf_op jit(solution)/shard_map/dot_general | solution.py:18
  477.3 35.5 %fusion.97 = f32[1,1536,128]{1,2,0:T(8,128)S(1)} fusion(f32[128,1536]{1,0:T(8,128)S(1)} %fusion, f32[2,1536,6144]{2,1,0:T(8,128)} %param.6, f32[1,2,6144,128]{3,2,1,0:T(8,128)S(1)} %copy-done.4), kind=kOutput, calls=%fused_computation.87 | convolution fusion | flops 14495711232 | bytes 42467328 | tf_op jit(solution)/shard_map/dot_general | solution.py:18
  512.8 35.0 %fusion.91 = f32[1,1536,128]{1,2,0:T(8,128)S(1)} fusion(f32[128,1536]{1,0:T(8,128)S(1)} %fusion.2, f32[2,1536,6144]{2,1,0:T(8,128)} %param.6, f32[1,2,6144,128]{3,2,1,0:T(8,128)S(1)} %copy-done.4), kind=kOutput, calls=%fused_computation.85 | convolution fusion | flops 14495711232 | bytes 42467328 | tf_op jit(solution)/shard_map/dot_general | solution.py:18
  547.9 1.2 pad_maximum_fusion.5
  549.1 36.3 %fusion.12 = f32[128,1536]{1,0:T(8,128)S(1)} fusion(f32[2,1536,6144]{2,1,0:T(8,128)} %param.6, f32[1,2,6144,128]{3,2,1,0:T(8,128)} %all-gather.9.cloned.1.call-done), kind=kOutput, calls=%fused_computation.17 | convolution fusion | flops 14495514624 | bytes 41680896 | tf_op jit(solution)/shard_map/dot_general | solution.py:18
  585.4 35.0 %fusion.14 = f32[128,1536]{1,0:T(8,128)S(1)} fusion(f32[2,1536,6144]{2,1,0:T(8,128)} %param.6, f32[1,2,6144,128]{3,2,1,0:T(8,128)S(1)} %copy-done.5), kind=kOutput, calls=%fused_computation.19 | convolution fusion | flops 14495514624 | bytes 41680896 | tf_op jit(solution)/shard_map/dot_general | solution.py:18
  620.5 35.5 %fusion.61 = f32[1,1536,128]{1,2,0:T(8,128)S(1)} fusion(f32[128,1536]{1,0:T(8,128)S(1)} %fusion.12, f32[2,1536,6144]{2,1,0:T(8,128)} %param.6, f32[1,2,6144,128]{3,2,1,0:T(8,128)S(1)} %copy-done.5), kind=kOutput, calls=%fused_computation.75 | convolution fusion | flops 14495711232 | bytes 42467328 | tf_op jit(solution)/shard_map/dot_general | solution.py:18
  655.9 35.0 %fusion.55 = f32[1,1536,128]{1,2,0:T(8,128)S(1)} fusion(f32[128,1536]{1,0:T(8,128)S(1)} %fusion.14, f32[2,1536,6144]{2,1,0:T(8,128)} %param.6, f32[1,2,6144,128]{3,2,1,0:T(8,128)S(1)} %copy-done.5), kind=kOutput, calls=%fused_computation.73 | convolution fusion | flops 14495711232 | bytes 42467328 | tf_op jit(solution)/shard_map/dot_general | solution.py:18
  691.0 1.3 pad_maximum_fusion.2
  692.4 1.6 dynamic-slice_multiply_fusion.2
  694.0 2.2 dynamic-slice_multiply_fusion.1
  696.2 2.3 dynamic-slice_multiply_fusion
  698.5 2.5 dynamic-slice_multiply_fusion.3
  701.1 2.9 pad_maximum_fusion.1
  704.5 1.7 gather_fusion.2
  708.2 1.5 broadcast_select_fusion
  709.7 13.4 %all-reduce.7.cloned.1.call-done = (f32[2,1536,128]{1,2,0:T(8,128)}, f32[2,1536,128]{1,2,0:T(8,128)}, f32[2,1536,128]{1,2,0:T(8,128)}, f32[2,1536,128]{1,2,0:T(8,128)}) async-done(((f32[2,1536,128]{1,2,0:T(8,128)}, f32[2,1536,128]{1,2,0:T(8,128)}, f32[2,1536,128]{1,2,0:T(8,128)}, f32[2,1536,128]{1,2,0:T(8,128)}), (f32[2,1536,128]{1,2,0:T(8,128)}, f32[2,1536,128]{1,2,0:T(8,128)}, f32[2,1536,128]{1,2,0:T(8,128)}, ...) | async-done | bytes 6291472 | tf_op jit(solution)/shard_map/psum | solution.py:66
  723.1 1.7 broadcast_multiply_fusion
  728.8 1.4 fusion.225
  730.2 1.4 fusion.224
  732.7 3.3 fusion.220
  740.9 0.9 fusion.51
  741.8 0.9 fusion.50
  742.7 0.9 fusion.49
  760.9 4.3 pad_maximum_fusion
  765.2 6.6 copy.33
  771.8 3.2 broadcast_in_dim.45
  775.0 13.3 %scatter_fusion = f32[4,2,1536,128]{3,2,1,0:T(8,128)} fusion(f32[4,2,1536,128]{3,2,1,0:T(8,128)} %broadcast_in_dim.45, s32[4]{0:T(128)S(1)} %copy-done.32, f32[4,2,1536,128]{3,2,1,0:T(8,128)} %copy.33), kind=kCustom, calls=%fused_computation.3 | custom fusion | bytes 18874384 | tf_op jit(solution)/shard_map/scatter | solution.py:118
  788.3 66.6 %all-reduce.5.cloned.1.call-done = (f32[4,2,128,128]{3,2,1,0:T(8,128)}, f32[2,2,128,128]{3,2,1,0:T(8,128)}) async-done(((f32[4,2,128,128]{3,2,1,0:T(8,128)}, f32[2,2,128,128]{3,2,1,0:T(8,128)}), (f32[4,2,128,128]{3,2,1,0:T(8,128)}, f32[2,2,128,128]{3,2,1,0:T(8,128)})) %all-reduce.5.cloned.1.call-update) | async-done | bytes 786448 | tf_op jit(solution)/shard_map/psum | solution.py:104
  854.9 1.1 slice_subtract_fusion.3
  857.7 1.0 fusion.140
  863.6 2.7 scatter_fusion.1
  (167 shorter events, 40.2 us)
Async XLA Ops:
  7.2 3.5 copy-start
  7.2 112.0 %all-gather.11.cloned.1.call-start = ((), (), s32[]{:S(2)}) async-start(), calls=%async_computation.1 | async-start | bytes 7077888 | tf_op jit(solution)/shard_map/all_gather | solution.py:64
  8.0 5.4 copy-start.33
  8.8 0.5 copy-start.31
  9.3 3.8 copy-start.30
  10.6 2.4 copy-start.34
  10.6 2.4 copy-start.36
  17.6 243.7 %all-gather.13.cloned.1.call-start = ((), (), s32[]{:S(2)}) async-start(), calls=%async_computation.2 | async-start | bytes 7077888 | tf_op jit(solution)/shard_map/all_gather | solution.py:64
  18.3 387.6 %all-gather.15.cloned.1.call-start = ((), (), s32[]{:S(2)}) async-start(), calls=%async_computation.3 | async-start | bytes 7077888 | tf_op jit(solution)/shard_map/all_gather | solution.py:64
  19.1 530.0 %all-gather.9.cloned.1.call-start = ((), (), s32[]{:S(2)}) async-start(), calls=%async_computation | async-start | bytes 7077888 | tf_op jit(solution)/shard_map/all_gather | solution.py:64
  19.7 703.5 %all-reduce.7.cloned.1.call-start = ((), (), s32[]{:S(2)}) async-start(), calls=%async_computation.5 | async-start | bytes 12582912 | tf_op jit(solution)/shard_map/psum | solution.py:66
  119.2 36.1 %copy-start.2 = (f32[1,2,6144,128]{3,2,1,0:T(8,128)S(1)}, f32[1,2,6144,128]{3,2,1,0:T(8,128)}, u32[]{:S(2)}) copy-start(f32[1,2,6144,128]{3,2,1,0:T(8,128)} %all-gather.11.cloned.1.call-done) | copy-start | bytes 18874372
  261.3 36.6 %copy-start.3 = (f32[1,2,6144,128]{3,2,1,0:T(8,128)S(1)}, f32[1,2,6144,128]{3,2,1,0:T(8,128)}, u32[]{:S(2)}) copy-start(f32[1,2,6144,128]{3,2,1,0:T(8,128)} %all-gather.13.cloned.1.call-done) | copy-start | bytes 18874372
  405.9 36.3 %copy-start.4 = (f32[1,2,6144,128]{3,2,1,0:T(8,128)S(1)}, f32[1,2,6144,128]{3,2,1,0:T(8,128)}, u32[]{:S(2)}) copy-start(f32[1,2,6144,128]{3,2,1,0:T(8,128)} %all-gather.15.cloned.1.call-done) | copy-start | bytes 18874372
  549.1 36.3 %copy-start.5 = (f32[1,2,6144,128]{3,2,1,0:T(8,128)S(1)}, f32[1,2,6144,128]{3,2,1,0:T(8,128)}, u32[]{:S(2)}) copy-start(f32[1,2,6144,128]{3,2,1,0:T(8,128)} %all-gather.9.cloned.1.call-done) | copy-start | bytes 18874372
  692.3 162.6 %all-reduce.5.cloned.1.call-start = ((), (), s32[]{:S(2)}) async-start(), calls=%async_computation.4 | async-start | bytes 1572864 | tf_op jit(solution)/shard_map/psum | solution.py:104
  694.0 7.1 copy-start.10
  696.2 4.9 copy-start.12
  698.5 5.5 copy-start.14
  701.1 3.4 copy-start.16
  701.1 5.2 copy-start.35
  701.1 5.2 copy-start.37
  701.1 6.4 copy-start.18
  704.5 27.2 %collective-permute-start = (f32[4,2,1536,128]{3,2,1,0:T(8,128)}, f32[4,2,1536,128]{3,2,1,0:T(8,128)}, u32[]{:S(2)}, u32[]{:S(2)}) collective-permute-start(f32[4,2,1536,128]{3,2,1,0:T(8,128)} %pad_maximum_fusion.1), channel_id=1, source_target_pairs={{0,1},{1,0},{2,3},{3,2},{4,5},{5,4},{6,7},{7,6},{8,9},{9,8},{10,11... | collective-permute-start | bytes 18874376 | tf_op jit(solution)/shard_map/ppermute | solution.py:14
  723.1 1.9 copy-start.19
  725.3 3.4 copy-start.20
  728.8 2.9 copy-start.11
  728.8 2.9 copy-start.13
  728.8 3.5 copy-start.15
  728.8 3.9 copy-start.17
  743.6 1.4 copy-start.23
  743.6 1.9 copy-start.24
  743.6 1.9 copy-start.28
  743.7 1.9 copy-start.29
  746.2 9.5 %copy-start.8 = (f32[2,1536,128]{1,2,0:T(8,128)}, f32[2,1536,128]{1,2,0:T(8,128)S(1)}, u32[]{:S(2)}) copy-start(f32[2,1536,128]{1,2,0:T(8,128)S(1)} %get-tuple-element.36) | copy-start | bytes 4718596
  746.2 11.1 %copy-start.6 = (f32[2,1536,128]{1,2,0:T(8,128)}, f32[2,1536,128]{1,2,0:T(8,128)S(1)}, u32[]{:S(2)}) copy-start(f32[2,1536,128]{1,2,0:T(8,128)S(1)} %get-tuple-element.35) | copy-start | bytes 4718596
  757.3 3.5 copy-start.9
  758.1 2.7 copy-start.7
  771.8 3.2 copy-start.32
  775.0 79.9 %copy-start.21 = (f32[4,2,128,128]{3,2,1,0:T(8,128)S(1)}, f32[4,2,128,128]{3,2,1,0:T(8,128)}, u32[]{:S(2)}) copy-start(f32[4,2,128,128]{3,2,1,0:T(8,128)} %broadcast_select_fusion) | copy-start | bytes 1572868
  788.3 70.4 %copy-start.26 = (f32[2,128,128]{1,2,0:T(8,128)S(1)}, f32[2,128,128]{1,2,0:T(8,128)}, u32[]{:S(2)}) copy-start(f32[2,128,128]{1,2,0:T(8,128)} %get-tuple-element.31) | copy-start | bytes 393220
  854.9 5.0 copy-start.27
  854.9 6.2 copy-start.22
  854.9 6.2 copy-start.25
  859.9 6.4 copy-start.1
Sparse Core Ops, SparseCore 0:
  17.7 101.4 all-gather.10
  121.4 96.8 all-gather.12
  220.5 96.9 all-gather.14
  320.1 96.8 all-gather.8
  692.4 30.6 all-reduce.6
  761.0 93.8 all-reduce.4
where the time goes:
time: 883 us; the launch traced here: 874 us
  matrix products  597 us (68%)
  waiting for transfers between devices  181 us (20%)
  other arithmetic  41.3 us (5%)
  local copies, waits for them, and re-layouts  38.3 us (4%)
  between operations  15.6 us (2%)
    dot_general x66, matrix products, matmul(): jnp.dot(left_side, right_side, preferred_element_type=jnp.float32, precis...  597 us
    all_gather x4, waiting for transfers between devices, per_device(): gathered = lax.all_gather(panels[tree_slot], 'row', axis=1, tiled=True)  99.5 us
    psum x1, waiting for transfers between devices, per_device(): lax.psum(jnp.stack(cross_local + child_local), ('row', 'col'))  66.6 us
  transfers between devices with their start and end apart: 7, of which 3 were waited for; matrix products, arithmetic and copies ran while one was open for 55% of the time, Pallas kernels for 0%

commit v1 on v0

--- a/solution.py
+++ b/solution.py
@@ -2,6 +2,11 @@
 import jax.numpy as jnp
 from jax import lax
 from jax.sharding import PartitionSpec as P
+
+
+def add_all(x, mesh_axis):
+    parts = lax.all_gather(x, mesh_axis)
+    return jnp.sum(parts, axis=0)
 
 
 def swapped(block, axis, bit):
@@ -101,7 +106,7 @@
     ]
     parent_sums = lax.psum(jnp.stack(parent_local), ("row", "col"))
     parent_diag = [diag_blocks[tree_slot] - parent_sums[tree_slot] for tree_slot in range(2)]
-    child_totals = lax.psum(jnp.stack(cross_local + child_local), ("row", "col"))
+    child_totals = add_all(jnp.stack(cross_local + child_local), ("row", "col"))
     crosses = [
         -(child_totals[tree_slot] + multiply(parent_diag[tree_slot], coupling[tree_slot]))
         for tree_slot in range(2)

time: 883 us -> 954 us (1.080)
  waiting for transfers between devices: 181 us -> 240 us
    all_gather x0 -> x1, waiting for transfers between devices: none -> 74.2 us  [add_all(): parts = lax.all_gather(x, mesh_axis)]
    psum x1, waiting for transfers between devices: 66.6 us -> 46.2 us  [per_device(): parent_sums = lax.psum(jnp.stack(parent_local), ('row', 'col'))]
  transfers between devices with their start and end apart: 7 -> 8, of which waited for: 3 -> 4; matrix products, arithmetic and copies ran while one was open for 55% -> 52% of each run, Pallas kernels for 0% -> 0%
where the time goes in v1:
time: 954 us; the launch traced here: 944 us
  matrix products  606 us (64%)
  waiting for transfers between devices  240 us (25%)
  other arithmetic  43.2 us (5%)
  local copies, waits for them, and re-layouts  39.3 us (4%)
  between operations  15.8 us (2%)
    dot_general x66, matrix products, matmul(): jnp.dot(left_side, right_side, preferred_element_type=jnp.float32, precis...  606 us
    all_gather x4, waiting for transfers between devices, per_device(): gathered = lax.all_gather(panels[tree_slot], 'row', axis=1, tiled=True)  99.5 us
    all_gather x1, waiting for transfers between devices, add_all(): parts = lax.all_gather(x, mesh_axis)  74.2 us
    psum x1, waiting for transfers between devices, per_device(): parent_sums = lax.psum(jnp.stack(parent_local), ('row', 'col'))  46.2 us
  transfers between devices with their start and end apart: 8, of which 4 were waited for; matrix products, arithmetic and copies ran while one was open for 52% of the time, Pallas kernels for 0%

profile of v1, /device:TPU:0, one launch (start us, length us, event | category | flops | bytes accessed | tf_op | source)
XLA Modules:
  0.0 944.4 jit_solution(13649763030751587616)
XLA Ops:
  10.7 2.4 gather_fusion.1
  13.5 2.4 select_multiply_fusion
  15.9 1.7 fusion.222
  19.8 99.5 %all-gather.13.cloned.1.call-done = f32[1,2,6144,128]{3,2,1,0:T(8,128)} async-done(((f32[1,2,768,128]{3,2,1,0:T(8,128)}), f32[1,2,6144,128]{3,2,1,0:T(8,128)}) %all-gather.13.cloned.1.call-update) | async-done | bytes 6291472 | tf_op jit(solution)/shard_map/all_gather | solution.py:69
  119.3 36.1 %fusion.8 = f32[128,1536]{1,0:T(8,128)S(1)} fusion(f32[2,1536,6144]{2,1,0:T(8,128)} %param.6, f32[1,2,6144,128]{3,2,1,0:T(8,128)} %all-gather.13.cloned.1.call-done), kind=kOutput, calls=%fused_computation.13 | convolution fusion | flops 14495514624 | bytes 41680896 | tf_op jit(solution)/shard_map/dot_general | solution.py:23
  155.4 35.0 %fusion.10 = f32[128,1536]{1,0:T(8,128)S(1)} fusion(f32[2,1536,6144]{2,1,0:T(8,128)} %param.6, f32[1,2,6144,128]{3,2,1,0:T(8,128)S(1)} %copy-done.2), kind=kOutput, calls=%fused_computation.15 | convolution fusion | flops 14495514624 | bytes 41680896 | tf_op jit(solution)/shard_map/dot_general | solution.py:23
  190.4 35.3 %fusion.73 = f32[1,1536,128]{1,2,0:T(8,128)S(1)} fusion(f32[128,1536]{1,0:T(8,128)S(1)} %fusion.8, f32[2,1536,6144]{2,1,0:T(8,128)} %param.6, f32[1,2,6144,128]{3,2,1,0:T(8,128)S(1)} %copy-done.2), kind=kOutput, calls=%fused_computation.79 | convolution fusion | flops 14495711232 | bytes 42467328 | tf_op jit(solution)/shard_map/dot_general | solution.py:23
  225.7 35.6 %fusion.67 = f32[1,1536,128]{1,2,0:T(8,128)S(1)} fusion(f32[128,1536]{1,0:T(8,128)S(1)} %fusion.10, f32[2,1536,6144]{2,1,0:T(8,128)} %param.6, f32[1,2,6144,128]{3,2,1,0:T(8,128)S(1)} %copy-done.2), kind=kOutput, calls=%fused_computation.77 | convolution fusion | flops 14495711232 | bytes 42467328 | tf_op jit(solution)/shard_map/dot_general | solution.py:23
  261.4 36.5 %fusion.4 = f32[128,1536]{1,0:T(8,128)S(1)} fusion(f32[2,1536,6144]{2,1,0:T(8,128)} %param.6, f32[1,2,6144,128]{3,2,1,0:T(8,128)} %all-gather.15.cloned.1.call-done), kind=kOutput, calls=%fused_computation.9 | convolution fusion | flops 14495514624 | bytes 41680896 | tf_op jit(solution)/shard_map/dot_general | solution.py:23
  297.9 35.2 %fusion.6 = f32[128,1536]{1,0:T(8,128)S(1)} fusion(f32[2,1536,6144]{2,1,0:T(8,128)} %param.6, f32[1,2,6144,128]{3,2,1,0:T(8,128)S(1)} %copy-done.3), kind=kOutput, calls=%fused_computation.11 | convolution fusion | flops 14495514624 | bytes 41680896 | tf_op jit(solution)/shard_map/dot_general | solution.py:23
  334.4 35.2 %fusion.85 = f32[1,1536,128]{1,2,0:T(8,128)S(1)} fusion(f32[128,1536]{1,0:T(8,128)S(1)} %fusion.4, f32[2,1536,6144]{2,1,0:T(8,128)} %param.6, f32[1,2,6144,128]{3,2,1,0:T(8,128)S(1)} %copy-done.3), kind=kOutput, calls=%fused_computation.83 | convolution fusion | flops 14495711232 | bytes 42467328 | tf_op jit(solution)/shard_map/dot_general | solution.py:23
  369.6 35.1 %fusion.79 = f32[1,1536,128]{1,2,0:T(8,128)S(1)} fusion(f32[128,1536]{1,0:T(8,128)S(1)} %fusion.6, f32[2,1536,6144]{2,1,0:T(8,128)} %param.6, f32[1,2,6144,128]{3,2,1,0:T(8,128)S(1)} %copy-done.3), kind=kOutput, calls=%fused_computation.81 | convolution fusion | flops 14495711232 | bytes 42467328 | tf_op jit(solution)/shard_map/dot_general | solution.py:23
  406.0 36.3 %fusion = f32[128,1536]{1,0:T(8,128)S(1)} fusion(f32[2,1536,6144]{2,1,0:T(8,128)} %param.6, f32[1,2,6144,128]{3,2,1,0:T(8,128)} %all-gather.17.cloned.1.call-done), kind=kOutput, calls=%fused_computation.5 | convolution fusion | flops 14495514624 | bytes 41680896 | tf_op jit(solution)/shard_map/dot_general | solution.py:23
  442.3 35.0 %fusion.2 = f32[128,1536]{1,0:T(8,128)S(1)} fusion(f32[2,1536,6144]{2,1,0:T(8,128)} %param.6, f32[1,2,6144,128]{3,2,1,0:T(8,128)S(1)} %copy-done.4), kind=kOutput, calls=%fused_computation.7 | convolution fusion | flops 14495514624 | bytes 41680896 | tf_op jit(solution)/shard_map/dot_general | solution.py:23
  477.3 35.5 %fusion.97 = f32[1,1536,128]{1,2,0:T(8,128)S(1)} fusion(f32[128,1536]{1,0:T(8,128)S(1)} %fusion, f32[2,1536,6144]{2,1,0:T(8,128)} %param.6, f32[1,2,6144,128]{3,2,1,0:T(8,128)S(1)} %copy-done.4), kind=kOutput, calls=%fused_computation.87 | convolution fusion | flops 14495711232 | bytes 42467328 | tf_op jit(solution)/shard_map/dot_general | solution.py:23
  512.8 35.0 %fusion.91 = f32[1,1536,128]{1,2,0:T(8,128)S(1)} fusion(f32[128,1536]{1,0:T(8,128)S(1)} %fusion.2, f32[2,1536,6144]{2,1,0:T(8,128)} %param.6, f32[1,2,6144,128]{3,2,1,0:T(8,128)S(1)} %copy-done.4), kind=kOutput, calls=%fused_computation.85 | convolution fusion | flops 14495711232 | bytes 42467328 | tf_op jit(solution)/shard_map/dot_general | solution.py:23
  549.1 36.3 %fusion.12 = f32[128,1536]{1,0:T(8,128)S(1)} fusion(f32[2,1536,6144]{2,1,0:T(8,128)} %param.6, f32[1,2,6144,128]{3,2,1,0:T(8,128)} %all-gather.11.cloned.1.call-done), kind=kOutput, calls=%fused_computation.17 | convolution fusion | flops 14495514624 | bytes 41680896 | tf_op jit(solution)/shard_map/dot_general | solution.py:23
  585.4 35.0 %fusion.14 = f32[128,1536]{1,0:T(8,128)S(1)} fusion(f32[2,1536,6144]{2,1,0:T(8,128)} %param.6, f32[1,2,6144,128]{3,2,1,0:T(8,128)S(1)} %copy-done.5), kind=kOutput, calls=%fused_computation.19 | convolution fusion | flops 14495514624 | bytes 41680896 | tf_op jit(solution)/shard_map/dot_general | solution.py:23
  620.5 35.5 %fusion.61 = f32[1,1536,128]{1,2,0:T(8,128)S(1)} fusion(f32[128,1536]{1,0:T(8,128)S(1)} %fusion.12, f32[2,1536,6144]{2,1,0:T(8,128)} %param.6, f32[1,2,6144,128]{3,2,1,0:T(8,128)S(1)} %copy-done.5), kind=kOutput, calls=%fused_computation.75 | convolution fusion | flops 14495711232 | bytes 42467328 | tf_op jit(solution)/shard_map/dot_general | solution.py:23
  655.9 35.0 %fusion.55 = f32[1,1536,128]{1,2,0:T(8,128)S(1)} fusion(f32[128,1536]{1,0:T(8,128)S(1)} %fusion.14, f32[2,1536,6144]{2,1,0:T(8,128)} %param.6, f32[1,2,6144,128]{3,2,1,0:T(8,128)S(1)} %copy-done.5), kind=kOutput, calls=%fused_computation.73 | convolution fusion | flops 14495711232 | bytes 42467328 | tf_op jit(solution)/shard_map/dot_general | solution.py:23
  692.4 1.6 dynamic-slice_multiply_fusion.2
  694.0 2.2 dynamic-slice_multiply_fusion.1
  696.1 2.3 dynamic-slice_multiply_fusion
  698.5 2.5 dynamic-slice_multiply_fusion.3
  701.0 3.0 pad_maximum_fusion.1
  705.2 17.9 %all-reduce.6.cloned.1.call-done = (f32[2,1536,128]{1,2,0:T(8,128)}, f32[2,1536,128]{1,2,0:T(8,128)}, f32[2,1536,128]{1,2,0:T(8,128)}, f32[2,1536,128]{1,2,0:T(8,128)}) async-done(((f32[2,1536,128]{1,2,0:T(8,128)}, f32[2,1536,128]{1,2,0:T(8,128)}, f32[2,1536,128]{1,2,0:T(8,128)}, f32[2,1536,128]{1,2,0:T(8,128)}), (f32[2,1536,128]{1,2,0:T(8,128)}, f32[2,1536,128]{1,2,0:T(8,128)}, f32[2,1536,128]{1,2,0:T(8,128)}, ...) | async-done | bytes 6291472 | tf_op jit(solution)/shard_map/psum | solution.py:71
  723.1 1.7 broadcast_multiply_fusion
  729.4 3.4 fusion.220
  743.6 1.6 fusion.135
  745.2 1.4 fusion.136
  746.7 1.4 fusion.133
  748.1 1.6 fusion.134
  755.5 1.8 fusion.110
  757.3 1.6 fusion.111
  758.9 1.8 fusion.106
  760.7 1.8 fusion.107
  762.6 1.8 fusion.108
  767.2 2.5 gather_fusion.2
  770.5 1.9 broadcast_select_fusion
  772.4 1.6 fusion.225
  774.2 3.2 pad_maximum_fusion
  777.4 6.6 copy.50
  784.0 3.2 broadcast_in_dim.45
  787.2 13.1 %scatter_fusion = f32[4,2,1536,128]{3,2,1,0:T(8,128)} fusion(f32[4,2,1536,128]{3,2,1,0:T(8,128)} %broadcast_in_dim.45, s32[4]{0:T(128)S(1)} %copy-done.46, f32[4,2,1536,128]{3,2,1,0:T(8,128)} %copy.50), kind=kCustom, calls=%fused_computation.3 | custom fusion | bytes 18874384 | tf_op jit(solution)/shard_map/scatter | solution.py:123
  800.3 46.2 %all-reduce.4.cloned.1.call-done = f32[2,2,128,128]{3,2,1,0:T(8,128)} async-done(((f32[2,2,128,128]{3,2,1,0:T(8,128)}), f32[2,2,128,128]{3,2,1,0:T(8,128)}) %all-reduce.4.cloned.1.call-update) | async-done | bytes 262160 | tf_op jit(solution)/shard_map/psum | solution.py:107
  849.2 74.2 %all-gather.19.cloned.1.call-done = f32[64,2,128,128]{3,2,1,0:T(8,128)} async-done(((f32[4,2,128,128]{3,2,1,0:T(8,128)}), f32[64,2,128,128]{3,2,1,0:T(8,128)}) %all-gather.19.cloned.1.call-update) | async-done | bytes 8388624 | tf_op jit(solution)/shard_map/all_gather | solution.py:8
  923.4 4.0 reduce_sum.9
  934.5 2.7 scatter_fusion.1
  (201 shorter events, 46.3 us)
Async XLA Ops:
  7.2 3.6 copy-start
  7.2 112.1 %all-gather.13.cloned.1.call-start = ((), (), s32[]{:S(2)}) async-start(), calls=%async_computation.2 | async-start | bytes 7077888 | tf_op jit(solution)/shard_map/all_gather | solution.py:69
  8.0 5.5 copy-start.47
  9.4 3.8 copy-start.44
  17.7 243.7 %all-gather.15.cloned.1.call-start = ((), (), s32[]{:S(2)}) async-start(), calls=%async_computation.3 | async-start | bytes 7077888 | tf_op jit(solution)/shard_map/all_gather | solution.py:69
  18.4 387.5 %all-gather.17.cloned.1.call-start = ((), (), s32[]{:S(2)}) async-start(), calls=%async_computation.4 | async-start | bytes 7077888 | tf_op jit(solution)/shard_map/all_gather | solution.py:69
  19.2 529.9 %all-gather.11.cloned.1.call-start = ((), (), s32[]{:S(2)}) async-start(), calls=%async_computation.1 | async-start | bytes 7077888 | tf_op jit(solution)/shard_map/all_gather | solution.py:69
  19.7 703.4 %all-reduce.6.cloned.1.call-start = ((), (), s32[]{:S(2)}) async-start(), calls=%async_computation.6 | async-start | bytes 12582912 | tf_op jit(solution)/shard_map/psum | solution.py:71
  119.3 36.1 %copy-start.2 = (f32[1,2,6144,128]{3,2,1,0:T(8,128)S(1)}, f32[1,2,6144,128]{3,2,1,0:T(8,128)}, u32[]{:S(2)}) copy-start(f32[1,2,6144,128]{3,2,1,0:T(8,128)} %all-gather.13.cloned.1.call-done) | copy-start | bytes 18874372
  261.4 36.6 %copy-start.3 = (f32[1,2,6144,128]{3,2,1,0:T(8,128)S(1)}, f32[1,2,6144,128]{3,2,1,0:T(8,128)}, u32[]{:S(2)}) copy-start(f32[1,2,6144,128]{3,2,1,0:T(8,128)} %all-gather.15.cloned.1.call-done) | copy-start | bytes 18874372
  406.0 36.3 %copy-start.4 = (f32[1,2,6144,128]{3,2,1,0:T(8,128)S(1)}, f32[1,2,6144,128]{3,2,1,0:T(8,128)}, u32[]{:S(2)}) copy-start(f32[1,2,6144,128]{3,2,1,0:T(8,128)} %all-gather.17.cloned.1.call-done) | copy-start | bytes 18874372
  549.1 36.3 %copy-start.5 = (f32[1,2,6144,128]{3,2,1,0:T(8,128)S(1)}, f32[1,2,6144,128]{3,2,1,0:T(8,128)}, u32[]{:S(2)}) copy-start(f32[1,2,6144,128]{3,2,1,0:T(8,128)} %all-gather.11.cloned.1.call-done) | copy-start | bytes 18874372
  692.3 154.2 %all-reduce.4.cloned.1.call-start = ((), (), s32[]{:S(2)}) async-start(), calls=%async_computation | async-start | bytes 524288 | tf_op jit(solution)/shard_map/psum | solution.py:107
  694.0 7.0 copy-start.10
  696.1 4.9 copy-start.12
  698.5 5.6 copy-start.14
  701.0 3.5 copy-start.50
  704.5 24.9 %collective-permute-start = (f32[4,2,1536,128]{3,2,1,0:T(8,128)}, f32[4,2,1536,128]{3,2,1,0:T(8,128)}, u32[]{:S(2)}, u32[]{:S(2)}) collective-permute-start(f32[4,2,1536,128]{3,2,1,0:T(8,128)} %pad_maximum_fusion.1), channel_id=1, source_target_pairs={{0,1},{1,0},{2,3},{3,2},{4,5},{5,4},{6,7},{7,6},{8,9},{9,8},{10,11... | collective-permute-start | bytes 18874376 | tf_op jit(solution)/shard_map/ppermute | solution.py:19
  725.9 11.1 %copy-start.23 = (f32[2,128,768]{2,1,0:T(8,128)}, f32[2,128,768]{2,1,0:T(8,128)S(1)}, u32[]{:S(2)}) copy-start(f32[2,128,768]{2,1,0:T(8,128)S(1)} %get-tuple-element.39) | copy-start | bytes 2359300
  725.9 24.3 %copy-start.21 = (f32[2,128,768]{2,1,0:T(8,128)}, f32[2,128,768]{2,1,0:T(8,128)S(1)}, u32[]{:S(2)}) copy-start(f32[2,128,768]{2,1,0:T(8,128)S(1)} %get-tuple-element.40) | copy-start | bytes 2359300
  725.9 3.5 copy-start.13
  725.9 3.5 copy-start.15
  726.0 3.5 copy-start.17
  733.2 8.7 copy-start.20
  733.2 17.0 %copy-start.18 = (f32[1,2,1536,128]{3,2,1,0:T(8,128)}, f32[1,2,1536,128]{3,2,1,0:T(8,128)S(1)}, u32[]{:S(2)}) copy-start(f32[1,2,1536,128]{3,2,1,0:T(8,128)S(1)} %get-tuple-element.13) | copy-start | bytes 4718596
  742.1 6.0 copy-start.24
  743.6 9.4 copy-start.6
  743.6 9.4 copy-start.8
  753.8 8.7 copy-start.7
  754.6 4.3 copy-start.9
  755.4 168.0 %all-gather.19.cloned.1.call-start = ((), (), s32[]{:S(2)}) async-start(), calls=%async_computation.5 | async-start | bytes 8912896 | tf_op jit(solution)/shard_map/all_gather | solution.py:8
  755.5 8.9 copy-start.25
  755.5 8.9 copy-start.42
  755.5 9.7 %copy-start.19 = (f32[1,2,1536,128]{3,2,1,0:T(8,128)S(1)}, f32[1,2,1536,128]{3,2,1,0:T(8,128)}, u32[]{:S(2)}) copy-start(f32[1,2,1536,128]{3,2,1,0:T(8,128)} %copy-done.18) | copy-start | bytes 4718596
  755.5 9.7 %copy-start.22 = (f32[2,128,768]{2,1,0:T(8,128)S(1)}, f32[2,128,768]{2,1,0:T(8,128)}, u32[]{:S(2)}) copy-start(f32[2,128,768]{2,1,0:T(8,128)} %copy-done.21) | copy-start | bytes 2359300
  755.5 10.2 %copy-start.43 = (f32[128,128]{1,0:T(8,128)S(1)}, f32[128,128]{1,0:T(8,128)}, u32[]{:S(2)}) copy-start(f32[128,128]{1,0:T(8,128)} %fusion.130) | copy-start | bytes 196612
  765.7 4.7 copy-start.48
  769.7 4.3 copy-start.29
  787.2 59.3 %copy-start.31 = (f32[4,2,128,128]{3,2,1,0:T(8,128)S(1)}, f32[4,2,128,128]{3,2,1,0:T(8,128)}, u32[]{:S(2)}) copy-start(f32[4,2,128,128]{3,2,1,0:T(8,128)} %broadcast_select_fusion) | copy-start | bytes 1572868
  847.5 80.0 %copy-start.32 = (f32[1,2,128,128]{3,2,1,0:T(8,128)}, f32[1,2,128,128]{3,2,1,0:T(8,128)S(1)}, u32[]{:S(2)}) copy-start(f32[1,2,128,128]{3,2,1,0:T(8,128)S(1)} %get-tuple-element.22) | copy-start | bytes 393220
  848.5 78.9 %copy-start.38 = (f32[128,128]{1,0:T(8,128)}, f32[128,128]{1,0:T(8,128)S(1)}, u32[]{:S(2)}) copy-start(f32[128,128]{1,0:T(8,128)S(1)} %convolution_add_fusion.5) | copy-start | bytes 196612
  848.8 78.7 %copy-start.39 = (f32[128,128]{1,0:T(8,128)}, f32[128,128]{1,0:T(8,128)S(1)}, u32[]{:S(2)}) copy-start(f32[128,128]{1,0:T(8,128)S(1)} %convolution_subtract_fusion.5) | copy-start | bytes 196612
  849.0 78.5 %copy-start.40 = (f32[128,128]{1,0:T(8,128)}, f32[128,128]{1,0:T(8,128)S(1)}, u32[]{:S(2)}) copy-start(f32[128,128]{1,0:T(8,128)S(1)} %convolution_add_fusion.3) | copy-start | bytes 196612
  849.2 78.3 %copy-start.41 = (f32[128,128]{1,0:T(8,128)}, f32[128,128]{1,0:T(8,128)S(1)}, u32[]{:S(2)}) copy-start(f32[128,128]{1,0:T(8,128)S(1)} %convolution_subtract_fusion.3) | copy-start | bytes 196612
  923.4 4.9 copy-start.37
  923.4 5.5 copy-start.36
  927.5 5.3 copy-start.33
  929.5 7.7 copy-start.1
  (13 other events, 29.1 us)
Sparse Core Ops, SparseCore 0:
  17.8 101.4 all-gather.12
  121.4 96.8 all-gather.14
  220.6 96.9 all-gather.16
  320.1 96.8 all-gather.10
  692.4 30.6 all-reduce.5
  755.5 90.8 all-reduce.3
  848.6 74.7 all-gather.18
